TPU v7x, 32 devices: a whole 2x2x4 slice. The times are simulated.
32 devices in a mesh: section: 2 (over x), dp: 4 (over z), expert: 4 (over y, core).
Axes of the slice: x: 2, y: 2, z: 4, core: 2. Of those that a mesh axis runs over, the one named last changes fastest.
Arguments:
- cotangent: bfloat16 [2, 128, 2048], P('section', ('dp', 'expert')), may hold values from -6 to 6
- routes: int32 [2, 1, 128, 8], P('section', None, ('dp', 'expert')), may hold values from 0 to 15, as said below
- probs: float32 [2, 1, 128, 8], P('section', None, ('dp', 'expert')), may hold values from 0.1 to 0.5
- stash: bfloat16 [2, 1, 4, 4, 4, 4, 8, 1536], P('section', None, 'dp', 'expert'), may hold values from -6 to 6
- w_gate: bfloat16 [2, 4, 4, 768, 2048], P('section', 'dp', 'expert'), may hold values from -0.125 to 0.125
- w_up: bfloat16 [2, 4, 4, 768, 2048], P('section', 'dp', 'expert'), may hold values from -0.125 to 0.125
- w_down: bfloat16 [2, 4, 4, 768, 2048], P('section', 'dp', 'expert'), may hold values from -0.21875 to 0.21875
Outputs:
- input_grads: bfloat16 [2, 128, 2048], P('section', ('dp', 'expert'))
Inputs may be any that keep to these rules, and one draw needn't show every extreme that they name: `routes`: within one section and stop, a token names 8 different experts, the tokens of one device name each expert at most 8 times, and some expert is named exactly 8 times by the tokens of every device.
All inputs are finite; a program needn't handle non-finite values.
Results may differ from a plain program's by a relative error of at most 0.012.
Values may be sent and summed in bfloat16 or wider, within the bound.
A program may use at most 64 MiB of HBM per device.

v0:
```python
import jax
import jax.numpy as jnp
from jax import lax
from jax.sharding import PartitionSpec as P


def shifted_2(value, axis, steps):
    count = lax.axis_size(axis)
    pairs = [(source, (source + steps) % count) for source in range(count)]
    return lax.ppermute(value, axis, pairs)


def body(cotangent, routes, probs, stash, w_gate, w_up, w_down):
    row_count = lax.axis_size("dp")
    column_count = lax.axis_size("expert")
    group_count = min(4, column_count)
    piece_count = column_count // group_count
    expert_count = group_count * row_count
    slot_most = stash.shape[6]
    model_width = w_gate.shape[4]
    piece_units = w_gate.shape[3]
    token_count = cotangent.shape[1]
    top_count = routes.shape[3]
    rows_dev = token_count * top_count
    code_count = expert_count * slot_most
    gate_piece = w_gate[0, 0, 0]
    up_piece = w_up[0, 0, 0]
    down_piece = w_down[0, 0, 0]
    earlier = lax.broadcasted_iota(jnp.int32, (rows_dev, rows_dev), 1) < lax.broadcasted_iota(
        jnp.int32, (rows_dev, rows_dev), 0
    )
    code_grid = lax.broadcasted_iota(jnp.int32, (rows_dev, code_count), 1)
    current = cotangent[0]
    shifted = shifted_2(current, "section", -1)
    expert_ids = routes[0, 0].reshape(-1)
    same_id = expert_ids[:, None] == expert_ids[None, :]
    ranked = jnp.sum(jnp.logical_and(same_id, earlier), axis=1)
    slot_code = expert_ids * slot_most + ranked
    selector = (slot_code[:, None] == code_grid).astype(jnp.bfloat16)
    grad_rows = (probs[0, 0][:, :, None] * shifted[:, None, :].astype(jnp.float32)).astype(
        jnp.bfloat16
    )
    grad_rows = grad_rows.reshape(rows_dev, model_width)
    packed = lax.dot_general(
        selector, grad_rows, (((0,), (0,)), ((), ())), preferred_element_type=jnp.float32
    )
    outgoing = packed.astype(jnp.bfloat16).reshape(group_count, row_count, slot_most, model_width)
    arrived = lax.all_to_all(outgoing, "dp", split_axis=1, concat_axis=1, tiled=True)
    copies = jnp.broadcast_to(
        arrived[:, None], (group_count, piece_count, row_count, slot_most, model_width)
    )
    copies = copies.reshape(column_count, row_count, slot_most, model_width)
    owned = lax.all_to_all(copies, "expert", split_axis=0, concat_axis=0, tiled=True)
    slot_rows = owned.reshape(-1, model_width)
    saved_pre = stash[0, 0, 0, 0].reshape(-1, 2 * piece_units)
    gate_pre = saved_pre[:, :piece_units].astype(jnp.float32)
    up_pre = saved_pre[:, piece_units:].astype(jnp.float32)
    grad_act = lax.dot_general(
        slot_rows, down_piece, (((1,), (1,)), ((), ())), preferred_element_type=jnp.float32
    )
    gate_sigmoid = jax.nn.sigmoid(gate_pre)
    grad_gate = (grad_act * up_pre * gate_sigmoid * (1.0 + gate_pre * (1.0 - gate_sigmoid))).astype(
        jnp.bfloat16
    )
    grad_up = (grad_act * gate_pre * gate_sigmoid).astype(jnp.bfloat16)
    partial_value = jnp.dot(grad_gate, gate_piece, preferred_element_type=jnp.float32)
    partial_value = (
        partial_value + jnp.dot(grad_up, up_piece, preferred_element_type=jnp.float32)
    ).astype(jnp.bfloat16)
    returned = lax.all_to_all(
        partial_value.reshape(column_count, row_count, slot_most, model_width),
        "expert",
        split_axis=0,
        concat_axis=0,
        tiled=True,
    )
    returned = returned.reshape(group_count, piece_count, row_count, slot_most, model_width)
    summed = jnp.sum(returned, axis=1, dtype=jnp.float32).astype(jnp.bfloat16)
    returned_rows = lax.all_to_all(summed, "dp", split_axis=1, concat_axis=1, tiled=True)
    token_select = jnp.sum(selector.reshape(token_count, top_count, code_count), axis=1)
    gathered = jnp.dot(
        token_select,
        returned_rows.reshape(code_count, model_width),
        preferred_element_type=jnp.float32,
    )
    current = (shifted.astype(jnp.float32) + gathered).astype(jnp.bfloat16)
    return current[None]


def solution(mesh):
    placed = (
        P("section", ("dp", "expert"), None),
        P("section", None, ("dp", "expert"), None),
        P("section", None, ("dp", "expert"), None),
        P("section", None, "dp", "expert", None, None, None, None),
        P("section", "dp", "expert", None, None),
        P("section", "dp", "expert", None, None),
        P("section", "dp", "expert", None, None),
    )
    return jax.shard_map(
        body,
        mesh=mesh,
        in_specs=placed,
        out_specs=P("section", ("dp", "expert"), None),
        check_vma=False,
    )
```

profile of v0, /device:TPU:0, one launch (start us, length us, event | category | flops | bytes accessed | tf_op | source)
XLA Modules:
  0.0 72.1 jit_solution(7368697439833427835)
XLA Ops:
  0.0 0.0 copy-start
  0.0 3.0 %collective-permute-start = (bf16[8,2048]{1,0:T(8,128)(2,1)}, bf16[8,2048]{1,0:T(8,128)(2,1)S(1)}, u32[]{:S(2)}, u32[]{:S(2)}) collective-permute-start(bf16[8,2048]{1,0:T(8,128)(2,1)} %bitcast.41), channel_id=1, source_target_pairs={{0,16},{16,0},{1,17},{17,1},{2,18},{18,2},{3,19},{19,3},{4,20},{20... | collective-permute-start | bytes 98312 | tf_op jit(solution)/shard_map/ppermute | solution.py:10
  3.0 0.8 %eq.28 = s32[64]{0:T(128)S(1)} reshape(s32[1,1,8,8]{3,2,1,0:T(8,128)} %param.8) | data formatting | bytes 512 | tf_op jit(solution)/shard_map/eq | solution.py:36
  3.7 0.2 convert_reduce_fusion
  3.9 0.8 %mul.59 = f32[64]{0:T(128)S(1)} reshape(f32[1,1,8,8]{3,2,1,0:T(8,128)} %param.9) | data formatting | bytes 512 | tf_op jit(solution)/shard_map/mul | solution.py:40
  4.7 0.0 copy-start.1
  4.7 0.4 collective-permute-done
  5.1 0.4 convolution_convert_fusion
  5.5 18.7 %all_to_all.20 = bf16[4,4,8,2048]{3,2,0,1:T(8,128)(2,1)S(1)} all-to-all(bf16[4,4,8,2048]{3,2,0,1:T(8,128)(2,1)S(1)} %copy.18), channel_id=1, replica_groups=mesh['section'=2,'dp'=4,'expert'=4] {'dp'}, dimensions={1} | all-to-all | bytes 1048576 | tf_op jit(solution)/shard_map/all_to_all | solution.py:48
  24.2 0.0 copy-start.2
  24.3 11.5 %all_to_all.21 = bf16[4,4,8,2048]{3,2,1,0:T(8,128)(2,1)S(1)} all-to-all(bf16[4,4,8,2048]{3,2,1,0:T(8,128)(2,1)S(1)} %copy.19), channel_id=1, replica_groups=mesh['section'=2,'dp'=4,'expert'=4] {'expert'}, dimensions={0} | all-to-all | bytes 1048576 | tf_op jit(solution)/shard_map/all_to_all | solution.py:53
  35.8 0.0 copy-done.1
  35.8 1.2 %fusion.4 = f32[128,768]{1,0:T(8,128)S(1)} fusion(bf16[128,2048]{1,0:T(8,128)(2,1)S(1)} %bitcast.37, bf16[1,1,1,768,2048]{4,3,2,1,0:T(8,128)(2,1)S(1)} %copy-done.1), kind=kOutput, calls=%fused_computation.4 | convolution fusion | flops 402653184 | bytes 4063232 | tf_op jit(solution)/shard_map/dot_general | solution.py:58
  37.0 0.0 copy-start.4
  37.0 0.0 copy-done
  37.0 0.0 copy-done.2
  37.0 0.6 fusion
  37.7 1.2 %copy-done.4 = bf16[1,1,1,768,2048]{4,3,2,1,0:T(8,128)(2,1)S(1)} copy-done((bf16[1,1,1,768,2048]{4,3,2,1,0:T(8,128)(2,1)S(1)}, bf16[1,1,1,768,2048]{4,3,2,1,0:T(8,128)(2,1)}, u32[]{:S(2)}) %copy-start.4) | copy-done | bytes 3145752
  38.9 0.0 copy-start.3
  38.9 0.7 fusion.9
  39.6 11.2 %all_to_all.22 = bf16[4,4,8,2048]{3,2,1,0:T(8,128)(2,1)S(1)} all-to-all(bf16[4,4,8,2048]{3,2,1,0:T(8,128)(2,1)S(1)} %bitcast.38), channel_id=1, replica_groups=mesh['section'=2,'dp'=4,'expert'=4] {'expert'}, dimensions={0} | all-to-all | bytes 1048576 | tf_op jit(solution)/shard_map/all_to_all | solution.py:70
  50.8 0.8 %copy.20 = bf16[4,4,8,2048]{3,2,0,1:T(8,128)(2,1)} copy(bf16[4,4,8,2048]{3,2,1,0:T(8,128)(2,1)S(1)} %all_to_all.22) | data formatting | bytes 1048576 | tf_op jit(solution)/shard_map/all_to_all | solution.py:70
  51.7 4.1 %all-to-all-start.3 = ((bf16[4,4,8,2048]{3,2,0,1:T(8,128)(2,1)}), bf16[4,4,8,2048]{3,2,0,1:T(8,128)(2,1)}, u32[]{:S(2)}, u32[]{:S(2)}) async-start(bf16[4,4,8,2048]{3,2,0,1:T(8,128)(2,1)} %copy.20), calls=%async_computation.3 | async-start | bytes 1048576 | tf_op jit(solution)/shard_map/all_to_all | solution.py:79
  55.8 0.1 reduce_sum.28
  55.9 0.0 copy-done.3
  55.9 0.1 fusion.35
  56.0 14.3 %all-to-all-done.3 = bf16[4,4,8,2048]{3,2,0,1:T(8,128)(2,1)} async-done(((bf16[4,4,8,2048]{3,2,0,1:T(8,128)(2,1)}), bf16[4,4,8,2048]{3,2,0,1:T(8,128)(2,1)}, u32[]{:S(2)}, u32[]{:S(2)}) %all-to-all-start.3) | async-done | bytes 524320 | tf_op jit(solution)/shard_map/all_to_all | solution.py:79
  70.3 1.1 %copy.21 = bf16[4,4,8,2048]{3,2,1,0:T(8,128)(2,1)S(1)} copy(bf16[4,4,8,2048]{3,2,0,1:T(8,128)(2,1)} %all-to-all-done.3) | data formatting | bytes 1048576 | tf_op jit(solution)/shard_map/all_to_all | solution.py:79
  71.3 0.8 %fusion.13 = bf16[1,8,2048]{2,1,0:T(8,128)(2,1)} fusion(bf16[8,128]{1,0:T(8,128)(2,1)S(1)} %fusion.35, bf16[128,2048]{1,0:T(8,128)(2,1)S(1)} %bitcast.36, bf16[8,2048]{1,0:T(8,128)(2,1)S(1)} %collective-permute-done), kind=kOutput, calls=%fused_computation.11 | convolution fusion | flops 4243456 | bytes 591872 | tf_op jit(solution)/shard_map/dot_general | solution.py:81
  (5 shorter events, 0.1 us)
Async XLA Ops:
  0.0 37.0 %copy-start = (bf16[1,1,1,768,2048]{4,3,2,1,0:T(8,128)(2,1)S(1)}, bf16[1,1,1,768,2048]{4,3,2,1,0:T(8,128)(2,1)}, u32[]{:S(2)}) copy-start(bf16[1,1,1,768,2048]{4,3,2,1,0:T(8,128)(2,1)} %param.12) | copy-start | bytes 9437188
  0.0 5.1 %collective-permute-start = (bf16[8,2048]{1,0:T(8,128)(2,1)}, bf16[8,2048]{1,0:T(8,128)(2,1)S(1)}, u32[]{:S(2)}, u32[]{:S(2)}) collective-permute-start(bf16[8,2048]{1,0:T(8,128)(2,1)} %bitcast.41), channel_id=1, source_target_pairs={{0,16},{16,0},{1,17},{17,1},{2,18},{18,2},{3,19},{19,3},{4,20},{20... | collective-permute-start | bytes 98312 | tf_op jit(solution)/shard_map/ppermute | solution.py:10
  4.7 31.1 %copy-start.1 = (bf16[1,1,1,768,2048]{4,3,2,1,0:T(8,128)(2,1)S(1)}, bf16[1,1,1,768,2048]{4,3,2,1,0:T(8,128)(2,1)}, u32[]{:S(2)}) copy-start(bf16[1,1,1,768,2048]{4,3,2,1,0:T(8,128)(2,1)} %param.13) | copy-start | bytes 9437188
  24.2 12.8 %copy-start.2 = (bf16[1,1,1,1,4,4,8,1536]{7,6,5,4,3,2,1,0:T(8,128)(2,1)S(1)}, bf16[1,1,1,1,4,4,8,1536]{7,6,5,4,3,2,1,0:T(8,128)(2,1)}, u32[]{:S(2)}) copy-start(bf16[1,1,1,1,4,4,8,1536]{7,6,5,4,3,2,1,0:T(8,128)(2,1)} %param.10) | copy-start | bytes 1179652
  37.0 1.9 %copy-start.4 = (bf16[1,1,1,768,2048]{4,3,2,1,0:T(8,128)(2,1)S(1)}, bf16[1,1,1,768,2048]{4,3,2,1,0:T(8,128)(2,1)}, u32[]{:S(2)}) copy-start(bf16[1,1,1,768,2048]{4,3,2,1,0:T(8,128)(2,1)} %param.11) | copy-start | bytes 9437188
  38.9 17.0 %copy-start.3 = (s32[1,1,8,8]{3,2,1,0:T(8,128)S(1)}, s32[1,1,8,8]{3,2,1,0:T(8,128)}, u32[]{:S(2)}) copy-start(s32[1,1,8,8]{3,2,1,0:T(8,128)} %param.8) | copy-start | bytes 772
  51.7 18.6 %all-to-all-start.3 = ((bf16[4,4,8,2048]{3,2,0,1:T(8,128)(2,1)}), bf16[4,4,8,2048]{3,2,0,1:T(8,128)(2,1)}, u32[]{:S(2)}, u32[]{:S(2)}) async-start(bf16[4,4,8,2048]{3,2,0,1:T(8,128)(2,1)} %copy.20), calls=%async_computation.3 | async-start | bytes 1048576 | tf_op jit(solution)/shard_map/all_to_all | solution.py:79
where the time goes:
time: 72.6 us; the launch traced here: 72.1 us
  blocking collectives  41.4 us (57%)
  waiting for transfers between devices  14.7 us (20%)
  starting transfers between devices  7.1 us (10%)
  local copies, waits for them, and re-layouts  4.85 us (7%)
  matrix products  3.73 us (5%)
    all_to_all x1, blocking collectives, body(): lax.all_to_all(outgoing, 'dp', split_axis=1, concat_axis=1, tiled=True)  18.7 us
    all_to_all x1, waiting for transfers between devices, body(): lax.all_to_all(summed, 'dp', split_axis=1, concat_axis=1, tiled=True)  14.3 us
    all_to_all x1, blocking collectives, body(): lax.all_to_all(copies, 'expert', split_axis=0, concat_axis=0, tiled=True)  11.5 us
    all_to_all x1, blocking collectives, body(): lax.all_to_all(partial_value.reshape(column_count, row_count, slot_most,...  11.2 us
    all_to_all x1, starting transfers between devices, body(): lax.all_to_all(summed, 'dp', split_axis=1, concat_axis=1, tiled=True)  4.13 us
    ppermute x1, starting transfers between devices, shifted_2(): return lax.ppermute(value, axis, pairs)  2.97 us
  transfers between devices with their start and end apart: 2, of which 2 were waited for; matrix products, arithmetic and copies ran while one was open for 3% of the time, Pallas kernels for 0%

commit v1 on v0

--- a/solution.py
+++ b/solution.py
@@ -1,7 +1,270 @@
+import functools
+
 import jax
 import jax.numpy as jnp
 from jax import lax
+from jax.experimental import pallas as pl
+from jax.experimental.pallas import tpu as pltpu
 from jax.sharding import PartitionSpec as P
+
+MESH = pl.DeviceIdType.MESH
+
+
+def relay_kernel(
+    sections, rows, columns, chunks,
+    cot, routes, probs, stash, gate_hbm, up_hbm, down_hbm, out,
+    tok, wt, stash_v, gate_v, up_v, down_v, obuf, r1, s1, r2, s2, r3,
+    load_sem, a_send, a_recv, y_send, y_recv, c_send, c_recv,
+    wz_send, wz_recv, wy_send, wy_recv, wc_send, wc_recv,
+    p1_send, p1_recv, p2_send, p2_recv, p3_send, p3_recv,
+):
+    sec = lax.axis_index("section")
+    row = lax.axis_index("dp")
+    col = lax.axis_index("expert")
+    core = lax.rem(col, 2)
+    ypos = col // 2
+    ycount = columns // 2
+    tokens, width = cot.shape
+    units = down_v.shape[0]
+    slots = columns * rows * tokens
+    chunk = width // chunks
+    mate = (sec, row, col + 1 - 2 * core)
+    before = lax.rem(sec + sections - 1, sections)
+    after = lax.rem(sec + 1, sections)
+
+    def zpeer(k):
+        return lax.rem(row + k, rows)
+
+    def zfrom(k):
+        return lax.rem(row + rows - k, rows)
+
+    def ypeer(j):
+        return lax.rem(col + 2 * j, columns)
+
+    def yfrom(j):
+        return lax.rem(col + columns - 2 * j, columns)
+
+    def remote(src, dst, send, recv, device):
+        return pltpu.make_async_remote_copy(
+            src_ref=src, dst_ref=dst, send_sem=send, recv_sem=recv,
+            device_id=device, device_id_type=MESH,
+        )
+
+    loads = [
+        pltpu.make_async_copy(stash, stash_v, load_sem.at[0]),
+        pltpu.make_async_copy(down_hbm, down_v, load_sem.at[1]),
+        pltpu.make_async_copy(gate_hbm, gate_v, load_sem.at[2]),
+        pltpu.make_async_copy(up_hbm, up_v, load_sem.at[3]),
+    ]
+
+    barrier = pltpu.get_barrier_semaphore()
+    greeted = 0
+    ring = [before] if sections == 2 else [before, after]
+    for other in ring:
+        for k in range(rows):
+            pl.semaphore_signal(barrier, inc=1, device_id=(other, zpeer(k), col), device_id_type=MESH)
+            greeted += 1
+    for k in range(1, rows):
+        pl.semaphore_signal(barrier, inc=1, device_id=(sec, zpeer(k), col), device_id_type=MESH)
+        greeted += 1
+    for j in range(1, ycount):
+        pl.semaphore_signal(barrier, inc=1, device_id=(sec, row, ypeer(j)), device_id_type=MESH)
+        greeted += 1
+    pl.semaphore_signal(barrier, inc=1, device_id=mate, device_id_type=MESH)
+    greeted += 1
+
+    for load in loads:
+        load.start()
+
+    lanes = wt.shape[3]
+    lane = lax.broadcasted_iota(jnp.int32, (tokens, lanes), 1)
+    tile = jnp.zeros((tokens, lanes), jnp.float32)
+    for k in range(routes.shape[1]):
+        tile = tile + jnp.where(routes[:, k:k + 1] == lane, probs[:, k:k + 1], 0.0)
+    wt[col, row] = tile
+
+    pl.semaphore_wait(barrier, greeted)
+
+    sends = []
+
+    def go(copy):
+        copy.start()
+        sends.append(copy)
+
+    def a_copy(k):
+        return remote(cot, tok.at[col, row], a_send.at[k], a_recv.at[k], (before, zpeer(k), col))
+
+    def a_wait(k):
+        src = zfrom(k)
+        remote(cot, tok.at[col, src], a_send.at[k], a_recv.at[k], mate).wait_recv()
+
+    for k in range(rows - 1, -1, -1):
+        go(a_copy(k))
+    for k in range(rows - 1, 0, -1):
+        go(remote(wt.at[col, row], wt.at[col, row], wz_send.at[k], wz_recv.at[k], (sec, zpeer(k), col)))
+
+    for k in range(rows - 1, 0, -1):
+        src = wt.at[col, zfrom(k)]
+        remote(src, src, wz_send.at[k], wz_recv.at[k], mate).wait_recv()
+    for j in range(1, ycount):
+        go(remote(wt.at[col], wt.at[col], wy_send.at[j], wy_recv.at[j], (sec, row, ypeer(j))))
+    go(remote(wt.at[col], wt.at[col], wc_send.at[0], wc_recv.at[0], mate))
+
+    for k in range(rows - 1, -1, -1):
+        a_wait(k)
+        block = tok.at[col, zfrom(k)]
+        for j in range(1, ycount):
+            go(remote(block, block, y_send.at[j, k], y_recv.at[j, k], (sec, row, ypeer(j))))
+        go(remote(block, block, c_send.at[0, k], c_recv.at[0, k], mate))
+
+    for j in range(1, ycount):
+        part = wt.at[yfrom(j)]
+        remote(part, part, wy_send.at[j], wy_recv.at[j], mate).wait_recv()
+        go(remote(part, part, wc_send.at[j], wc_recv.at[j], mate))
+    for k in range(rows - 1, -1, -1):
+        for j in range(1, ycount):
+            block = tok.at[yfrom(j), zfrom(k)]
+            remote(block, block, y_send.at[j, k], y_recv.at[j, k], mate).wait_recv()
+            go(remote(block, block, c_send.at[j, k], c_recv.at[j, k], mate))
+    mate_col = col + 1 - 2 * core
+    for j in range(ycount):
+        part = wt.at[lax.rem(mate_col + columns - 2 * j, columns)]
+        remote(part, part, wc_send.at[j], wc_recv.at[j], mate).wait_recv()
+
+    expert = col * rows + row
+    weights = wt[...].reshape(slots, lanes)
+    wide = lax.broadcasted_iota(jnp.int32, (slots, lanes), 1)
+    weight = jnp.sum(jnp.where(wide == expert, weights, 0.0), axis=1, keepdims=True)
+    named = jnp.broadcast_to((weight > 0.0).astype(jnp.float32), (slots, slots))
+    at_row = lax.broadcasted_iota(jnp.int32, (slots, slots), 0)
+    at_col = lax.broadcasted_iota(jnp.int32, (slots, slots), 1)
+    same = (at_row // tokens) == (at_col // tokens)
+    lower = jnp.where(jnp.logical_and(same, at_col < at_row), 1.0, 0.0).astype(jnp.bfloat16)
+    rank = jnp.dot(lower, named.astype(jnp.bfloat16), preferred_element_type=jnp.float32)
+    spot = ((at_row // tokens) * tokens).astype(jnp.float32) + rank
+    pick = jnp.where(at_col.astype(jnp.float32) == spot, named, 0.0).astype(jnp.bfloat16)
+    loads[0].wait()
+    saved = stash_v[...].astype(jnp.float32).reshape(slots, 2 * units).astype(jnp.bfloat16)
+    saved = jnp.dot(pick, saved, preferred_element_type=jnp.float32)
+    gate_pre = saved[:, :units]
+    up_pre = saved[:, units:]
+    sg = jax.nn.sigmoid(gate_pre)
+    f_gate = up_pre * sg * (1.0 + gate_pre * (1.0 - sg))
+    f_up = gate_pre * sg
+    loads[1].wait()
+
+    for k in range(rows - 1, -1, -1):
+        for j in range(ycount):
+            block = tok.at[lax.rem(mate_col + columns - 2 * j, columns), zfrom(k)]
+            remote(block, block, c_send.at[j, k], c_recv.at[j, k], mate).wait_recv()
+
+    moved = tok[...].astype(jnp.float32).reshape(slots, width)
+    grad_rows = (moved * weight).astype(jnp.bfloat16)
+    grad_act = lax.dot_general(
+        grad_rows, down_v[...], (((1,), (1,)), ((), ())), preferred_element_type=jnp.float32
+    )
+    grad_gate = (grad_act * f_gate).astype(jnp.bfloat16)
+    grad_up = (grad_act * f_up).astype(jnp.bfloat16)
+    loads[2].wait()
+    loads[3].wait()
+
+    def p1(t):
+        return remote(obuf.at[t, 1 - core], r1.at[t], p1_send.at[t], p1_recv.at[t], mate)
+
+    def p2(t, j):
+        return remote(s1.at[t, j], r2.at[t, j], p2_send.at[t, j], p2_recv.at[t, j], (sec, row, ypeer(j)))
+
+    def p3(t, k):
+        return remote(s2.at[t, k], r3.at[t, k], p3_send.at[t, k], p3_recv.at[t, k], (sec, zpeer(k), col))
+
+    def f32(value):
+        return value.astype(jnp.float32)
+
+    for t in range(chunks):
+        span = slice(t * chunk, (t + 1) * chunk)
+        part = jnp.dot(grad_gate, gate_v[:, span], preferred_element_type=jnp.float32)
+        part = part + jnp.dot(grad_up, up_v[:, span], preferred_element_type=jnp.float32)
+        part = part.reshape(ycount, 2, rows, tokens, chunk).astype(jnp.bfloat16)
+        obuf[t, 0] = part[:, 0]
+        obuf[t, 1] = part[:, 1]
+        go(p1(t))
+    for t in range(chunks):
+        p1(t).wait_recv()
+        for j in range(1, ycount):
+            y = lax.rem(ypos + j, ycount)
+            s1[t, j] = (f32(obuf[t, core, y]) + f32(r1[t, y])).astype(jnp.bfloat16)
+            go(p2(t, j))
+    for t in range(chunks):
+        for j in range(1, ycount):
+            p2(t, j).wait_recv()
+        for k in range(rows - 1, 0, -1):
+            to = zpeer(k)
+            total = f32(obuf[t, core, ypos, to]) + f32(r1[t, ypos, to])
+            for j in range(1, ycount):
+                total = total + f32(r2[t, j, to])
+            s2[t, k] = total.astype(jnp.bfloat16)
+            go(p3(t, k))
+    for t in range(chunks):
+        span = slice(t * chunk, (t + 1) * chunk)
+        total = f32(obuf[t, core, ypos, row]) + f32(r1[t, ypos, row])
+        for j in range(1, ycount):
+            total = total + f32(r2[t, j, row])
+        for k in range(rows - 1, 0, -1):
+            p3(t, k).wait_recv()
+            total = total + f32(r3[t, k])
+        out[:, span] = (f32(tok[col, row, :, span]) + total).astype(jnp.bfloat16)
+    for copy in sends:
+        copy.wait_send()
+
+
+def relay(mesh, cotangent, routes, probs, stash, w_gate, w_up, w_down):
+    sections, rows, columns = (mesh.shape[name] for name in ("section", "dp", "expert"))
+    tokens, width = cotangent.shape[1:]
+    units = w_gate.shape[3]
+    ycount = columns // 2
+    lanes = -(-rows * columns // 128) * 128
+    chunks = max(width // 512, 1)
+    chunk = width // chunks
+    bf16 = jnp.bfloat16
+    dma = pltpu.SemaphoreType.DMA
+    vmem = pl.BlockSpec(memory_space=pltpu.VMEM)
+    hbm = pl.BlockSpec(memory_space=pl.ANY)
+    out = pl.pallas_call(
+        functools.partial(relay_kernel, sections, rows, columns, chunks),
+        out_shape=jax.ShapeDtypeStruct((tokens, width), bf16),
+        in_specs=[hbm, vmem, vmem, hbm, hbm, hbm, hbm],
+        out_specs=vmem,
+        scratch_shapes=[
+            pltpu.VMEM((columns, rows, tokens, width), bf16),
+            pltpu.VMEM((columns, rows, tokens, lanes), jnp.float32),
+            pltpu.VMEM((columns, rows, tokens, 2 * units), bf16),
+            pltpu.VMEM((units, width), bf16),
+            pltpu.VMEM((units, width), bf16),
+            pltpu.VMEM((units, width), bf16),
+            pltpu.VMEM((chunks, 2, ycount, rows, tokens, chunk), bf16),
+            pltpu.VMEM((chunks, ycount, rows, tokens, chunk), bf16),
+            pltpu.VMEM((chunks, ycount, rows, tokens, chunk), bf16),
+            pltpu.VMEM((chunks, ycount, rows, tokens, chunk), bf16),
+            pltpu.VMEM((chunks, rows, tokens, chunk), bf16),
+            pltpu.VMEM((chunks, rows, tokens, chunk), bf16),
+            dma((4,)),
+            dma((rows,)), dma((rows,)),
+            dma((ycount, rows)), dma((ycount, rows)),
+            dma((ycount, rows)), dma((ycount, rows)),
+            dma((rows,)), dma((rows,)),
+            dma((ycount,)), dma((ycount,)),
+            dma((ycount,)), dma((ycount,)),
+            dma((chunks,)), dma((chunks,)),
+            dma((chunks, ycount)), dma((chunks, ycount)),
+            dma((chunks, rows)), dma((chunks, rows)),
+        ],
+        compiler_params=pltpu.CompilerParams(collective_id=0, has_side_effects=True),
+    )(
+        cotangent[0], routes[0, 0], probs[0, 0],
+        stash.reshape(columns, rows, tokens, 2 * units),
+        w_gate[0, 0, 0], w_up[0, 0, 0], w_down[0, 0, 0],
+    )
+    return out[None]
 
 
 def shifted_2(value, axis, steps):
@@ -10,7 +273,12 @@
     return lax.ppermute(value, axis, pairs)
 
 
-def body(cotangent, routes, probs, stash, w_gate, w_up, w_down):
+def body(mesh, cotangent, routes, probs, stash, w_gate, w_up, w_down):
+    if (
+        mesh.shape["expert"] in (2, 4)
+        and stash.shape[6] == cotangent.shape[1]
+    ):
+        return relay(mesh, cotangent, routes, probs, stash, w_gate, w_up, w_down)
     row_count = lax.axis_size("dp")
     column_count = lax.axis_size("expert")
     group_count = min(4, column_count)
@@ -98,7 +366,7 @@
         P("section", "dp", "expert", None, None),
     )
     return jax.shard_map(
-        body,
+        functools.partial(body, mesh),
         mesh=mesh,
         in_specs=placed,
         out_specs=P("section", ("dp", "expert"), None),

time: 72.6 us -> 32.3 us (0.44)
  blocking collectives: 41.4 us -> 0 us
  Pallas kernels: 0 us -> 30.7 us
  waiting for transfers between devices: 14.7 us -> 0 us
  starting transfers between devices: 7.1 us -> 0 us
  matrix products: 3.73 us -> 0 us
  local copies, waits for them, and re-layouts: 4.85 us -> 1.38 us
    all_to_all x3 -> x0, blocking collectives: 41.4 us -> none  [the longest x1 18.7 us: body(): lax.all_to_all(outgoing, 'dp', split_axis=1, concat_axis=1, tiled=True)]
    pallas_call x0 -> x1, Pallas kernels: none -> 30.7 us  [relay(): pl.pallas_call(functools.partial(relay_kernel, sections, rows, columns, c...]
    all_to_all x1 -> x0, waiting for transfers between devices: 14.3 us -> none  [body(): lax.all_to_all(summed, 'dp', split_axis=1, concat_axis=1, tiled=True)]
    all_to_all x1 -> x0, starting transfers between devices: 4.13 us -> none  [body(): lax.all_to_all(summed, 'dp', split_axis=1, concat_axis=1, tiled=True)]
    dot_general x5 -> x0, matrix products: 3.73 us -> none  [the longest x1 1.17 us: body(): lax.dot_general(slot_rows, down_piece, (((1,), (1,)), ((), ())), preferre...]
    ppermute x1 -> x0, starting transfers between devices: 2.97 us -> none  [shifted_2(): return lax.ppermute(value, axis, pairs)]
    all_to_all x3 -> x0, local copies, waits for them, and re-layouts: 1.95 us -> none  [the longest x1 1.08 us: body(): lax.all_to_all(summed, 'dp', split_axis=1, concat_axis=1, tiled=True)]
    mul x1 -> x0, local copies, waits for them, and re-layouts: 0.77 us -> none  [body(): probs[0, 0][:, :, None] * shifted[:, None, :].astype(jnp.float32)]
  transfers between devices with their start and end apart: 2 -> 0, of which waited for: 2 -> 0; matrix products, arithmetic and copies ran while one was open for 3% -> 0% of each run, Pallas kernels for 0% -> 0%
where the time goes in v1:
time: 32.3 us; the launch traced here: 32.1 us
  Pallas kernels  30.7 us (95%)
  local copies, waits for them, and re-layouts  1.38 us (4%)
    pallas_call x1, Pallas kernels, relay(): pl.pallas_call(functools.partial(relay_kernel, sections, rows, columns, c...  30.7 us
    unnamed x1, local copies, waits for them, and re-layouts  1.38 us

profile of v1, /device:TPU:0, one launch (start us, length us, event | category | flops | bytes accessed | tf_op | source)
XLA Modules:
  0.0 32.1 jit_solution(11143038787716290507)
XLA Ops:
  0.0 30.7 %shard_map.73 = bf16[8,2048]{1,0:T(8,128)(2,1)} custom-call(bf16[8,2048]{1,0:T(8,128)(2,1)} %bitcast.13, s32[8,8]{1,0:T(8,128)} %bitcast.14, f32[8,8]{1,0:T(8,128)} %bitcast.15, bf16[4,4,8,1536]{3,2,1,0:T(8,128)(2,1)} %bitcast.11, bf16[768,2048]{1,0:T(8,128)(2,1)} %bitcast.8, bf16[768,2048]{1,0:T(8,128)(2,1)} %bitcast.9, bf16[768,2048]{1,0:T(8,128)(2,1)} %bitcast.10), custom_call_target="tpu_custom_call" | custom-call | tf_op jit(solution)/shard_map/pallas_call | solution.py:232
  30.7 1.4 %copy.9 = bf16[1,8,2048]{2,1,0:T(8,128)(2,1)} copy(bf16[1,8,2048]{2,1,0:T(8,128)(2,1)} %bitcast.12) | data formatting | bytes 65536

commit v2 on v1

--- a/solution.py
+++ b/solution.py
@@ -12,8 +12,8 @@
 
 def relay_kernel(
     sections, rows, columns, chunks,
-    cot, routes, probs, stash, gate_hbm, up_hbm, down_hbm, out,
-    tok, wt, stash_v, gate_v, up_v, down_v, obuf, r1, s1, r2, s2, r3,
+    cot, routes_hbm, probs_hbm, stash, gate_hbm, up_hbm, down_hbm, out,
+    routes, probs, tok, wt, stash_v, gate_v, up_v, down_v, obuf, r1, s1, r2, s2, r3,
     load_sem, a_send, a_recv, y_send, y_recv, c_send, c_recv,
     wz_send, wz_recv, wy_send, wy_recv, wc_send, wc_recv,
     p1_send, p1_recv, p2_send, p2_recv, p3_send, p3_recv,
@@ -50,6 +50,10 @@
             device_id=device, device_id_type=MESH,
         )
 
+    small = [
+        pltpu.make_async_copy(routes_hbm, routes, load_sem.at[4]),
+        pltpu.make_async_copy(probs_hbm, probs, load_sem.at[5]),
+    ]
     loads = [
         pltpu.make_async_copy(stash, stash_v, load_sem.at[0]),
         pltpu.make_async_copy(down_hbm, down_v, load_sem.at[1]),
@@ -57,6 +61,8 @@
         pltpu.make_async_copy(up_hbm, up_v, load_sem.at[3]),
     ]
 
+    for load in small:
+        load.start()
     barrier = pltpu.get_barrier_semaphore()
     greeted = 0
     ring = [before] if sections == 2 else [before, after]
@@ -76,6 +82,8 @@
     for load in loads:
         load.start()
 
+    for load in small:
+        load.wait()
     lanes = wt.shape[3]
     lane = lax.broadcasted_iota(jnp.int32, (tokens, lanes), 1)
     tile = jnp.zeros((tokens, lanes), jnp.float32)
@@ -231,10 +239,12 @@
     hbm = pl.BlockSpec(memory_space=pl.ANY)
     out = pl.pallas_call(
         functools.partial(relay_kernel, sections, rows, columns, chunks),
-        out_shape=jax.ShapeDtypeStruct((tokens, width), bf16),
-        in_specs=[hbm, vmem, vmem, hbm, hbm, hbm, hbm],
+        out_shape=pltpu.VMEM((tokens, width), bf16),
+        in_specs=[hbm, hbm, hbm, hbm, hbm, hbm, hbm],
         out_specs=vmem,
         scratch_shapes=[
+            pltpu.VMEM(routes.shape[2:], jnp.int32),
+            pltpu.VMEM(probs.shape[2:], jnp.float32),
             pltpu.VMEM((columns, rows, tokens, width), bf16),
             pltpu.VMEM((columns, rows, tokens, lanes), jnp.float32),
             pltpu.VMEM((columns, rows, tokens, 2 * units), bf16),
@@ -247,7 +257,7 @@
             pltpu.VMEM((chunks, ycount, rows, tokens, chunk), bf16),
             pltpu.VMEM((chunks, rows, tokens, chunk), bf16),
             pltpu.VMEM((chunks, rows, tokens, chunk), bf16),
-            dma((4,)),
+            dma((6,)),
             dma((rows,)), dma((rows,)),
             dma((ycount, rows)), dma((ycount, rows)),
             dma((ycount, rows)), dma((ycount, rows)),

time: 32.3 us -> 30.2 us (0.935)
  Pallas kernels: 30.7 us -> 29.4 us
  local copies, waits for them, and re-layouts: 1.38 us -> 0.62 us
    pallas_call x1, Pallas kernels: 30.7 us -> 29.4 us  [relay(): pl.pallas_call(functools.partial(relay_kernel, sections, rows, columns, c...]
    unnamed x1, local copies, waits for them, and re-layouts: 1.38 us -> 0.62 us
where the time goes in v2:
time: 30.2 us; the launch traced here: 30 us
  Pallas kernels  29.4 us (97%)
  local copies, waits for them, and re-layouts  0.62 us (2%)
    pallas_call x1, Pallas kernels, relay(): pl.pallas_call(functools.partial(relay_kernel, sections, rows, columns, c...  29.4 us
    unnamed x1, local copies, waits for them, and re-layouts  0.62 us

profile of v2, /device:TPU:0, one launch (start us, length us, event | category | flops | bytes accessed | tf_op | source)
XLA Modules:
  0.0 30.0 jit_solution(9503969283573285658)
XLA Ops:
  0.0 29.4 %shard_map.73 = bf16[8,2048]{1,0:T(8,128)(2,1)S(1)} custom-call(bf16[8,2048]{1,0:T(8,128)(2,1)} %bitcast.13, s32[8,8]{1,0:T(8,128)} %bitcast.14, f32[8,8]{1,0:T(8,128)} %bitcast.15, bf16[4,4,8,1536]{3,2,1,0:T(8,128)(2,1)} %bitcast.12, bf16[768,2048]{1,0:T(8,128)(2,1)} %bitcast.9, bf16[768,2048]{1,0:T(8,128)(2,1)} %bitcast.10, bf16[768,2048]{1,0:T(8,128)(2,1)} %bitcast.11), custom_call_target="tpu_custom_call" | custom-call | tf_op jit(solution)/shard_map/pallas_call | solution.py:240
  29.4 0.6 %copy.9 = bf16[1,8,2048]{2,1,0:T(8,128)(2,1)} copy(bf16[1,8,2048]{2,1,0:T(8,128)(2,1)S(1)} %bitcast.8) | data formatting | bytes 65536

commit v3 on v2

--- a/solution.py
+++ b/solution.py
@@ -12,8 +12,8 @@
 
 def relay_kernel(
     sections, rows, columns, chunks,
-    cot, routes_hbm, probs_hbm, stash, gate_hbm, up_hbm, down_hbm, out,
-    routes, probs, tok, wt, stash_v, gate_v, up_v, down_v, obuf, r1, s1, r2, s2, r3,
+    cot_hbm, routes_hbm, probs_hbm, stash, gate_hbm, up_hbm, down_hbm, out,
+    cot, routes, probs, tok, wt, stash_v, gate_v, up_v, down_v, obuf, r1, s1, r2, s2, r3,
     load_sem, a_send, a_recv, y_send, y_recv, c_send, c_recv,
     wz_send, wz_recv, wy_send, wy_recv, wc_send, wc_recv,
     p1_send, p1_recv, p2_send, p2_recv, p3_send, p3_recv,
@@ -51,6 +51,7 @@
         )
 
     small = [
+        pltpu.make_async_copy(cot_hbm, cot, load_sem.at[6]),
         pltpu.make_async_copy(routes_hbm, routes, load_sem.at[4]),
         pltpu.make_async_copy(probs_hbm, probs, load_sem.at[5]),
     ]
@@ -231,7 +232,7 @@
     units = w_gate.shape[3]
     ycount = columns // 2
     lanes = -(-rows * columns // 128) * 128
-    chunks = max(width // 512, 1)
+    chunks = max(width // 1024, 1)
     chunk = width // chunks
     bf16 = jnp.bfloat16
     dma = pltpu.SemaphoreType.DMA
@@ -243,6 +244,7 @@
         in_specs=[hbm, hbm, hbm, hbm, hbm, hbm, hbm],
         out_specs=vmem,
         scratch_shapes=[
+            pltpu.VMEM((tokens, width), bf16),
             pltpu.VMEM(routes.shape[2:], jnp.int32),
             pltpu.VMEM(probs.shape[2:], jnp.float32),
             pltpu.VMEM((columns, rows, tokens, width), bf16),
@@ -257,7 +259,7 @@
             pltpu.VMEM((chunks, ycount, rows, tokens, chunk), bf16),
             pltpu.VMEM((chunks, rows, tokens, chunk), bf16),
             pltpu.VMEM((chunks, rows, tokens, chunk), bf16),
-            dma((6,)),
+            dma((7,)),
             dma((rows,)), dma((rows,)),
             dma((ycount, rows)), dma((ycount, rows)),
             dma((ycount, rows)), dma((ycount, rows)),

time: 30.2 us -> 29.3 us (0.970)
  Pallas kernels: 29.4 us -> 28.5 us
    pallas_call x1, Pallas kernels: 29.4 us -> 28.5 us  [relay(): pl.pallas_call(functools.partial(relay_kernel, sections, rows, columns, c...]
where the time goes in v3:
time: 29.3 us; the launch traced here: 29.2 us
  Pallas kernels  28.5 us (97%)
  local copies, waits for them, and re-layouts  0.62 us (2%)
    pallas_call x1, Pallas kernels, relay(): pl.pallas_call(functools.partial(relay_kernel, sections, rows, columns, c...  28.5 us
    unnamed x1, local copies, waits for them, and re-layouts  0.62 us

profile of v3, /device:TPU:0, one launch (start us, length us, event | category | flops | bytes accessed | tf_op | source)
XLA Modules:
  0.0 29.2 jit_solution(2840365845635524069)
XLA Ops:
  0.0 28.5 %shard_map.73 = bf16[8,2048]{1,0:T(8,128)(2,1)S(1)} custom-call(bf16[8,2048]{1,0:T(8,128)(2,1)} %bitcast.13, s32[8,8]{1,0:T(8,128)} %bitcast.14, f32[8,8]{1,0:T(8,128)} %bitcast.15, bf16[4,4,8,1536]{3,2,1,0:T(8,128)(2,1)} %bitcast.12, bf16[768,2048]{1,0:T(8,128)(2,1)} %bitcast.9, bf16[768,2048]{1,0:T(8,128)(2,1)} %bitcast.10, bf16[768,2048]{1,0:T(8,128)(2,1)} %bitcast.11), custom_call_target="tpu_custom_call" | custom-call | tf_op jit(solution)/shard_map/pallas_call | solution.py:241
  28.6 0.6 %copy.9 = bf16[1,8,2048]{2,1,0:T(8,128)(2,1)} copy(bf16[1,8,2048]{2,1,0:T(8,128)(2,1)S(1)} %bitcast.8) | data formatting | bytes 65536

commit v4 on v3

--- a/solution.py
+++ b/solution.py
@@ -112,19 +112,19 @@
     for k in range(rows - 1, 0, -1):
         go(remote(wt.at[col, row], wt.at[col, row], wz_send.at[k], wz_recv.at[k], (sec, zpeer(k), col)))
 
-    for k in range(rows - 1, 0, -1):
-        src = wt.at[col, zfrom(k)]
-        remote(src, src, wz_send.at[k], wz_recv.at[k], mate).wait_recv()
-    for j in range(1, ycount):
-        go(remote(wt.at[col], wt.at[col], wy_send.at[j], wy_recv.at[j], (sec, row, ypeer(j))))
-    go(remote(wt.at[col], wt.at[col], wc_send.at[0], wc_recv.at[0], mate))
-
-    for k in range(rows - 1, -1, -1):
+    for k in range(rows):
         a_wait(k)
         block = tok.at[col, zfrom(k)]
         for j in range(1, ycount):
             go(remote(block, block, y_send.at[j, k], y_recv.at[j, k], (sec, row, ypeer(j))))
         go(remote(block, block, c_send.at[0, k], c_recv.at[0, k], mate))
+        if k == 0:
+            for n in range(rows - 1, 0, -1):
+                src = wt.at[col, zfrom(n)]
+                remote(src, src, wz_send.at[n], wz_recv.at[n], mate).wait_recv()
+            for j in range(1, ycount):
+                go(remote(wt.at[col], wt.at[col], wy_send.at[j], wy_recv.at[j], (sec, row, ypeer(j))))
+            go(remote(wt.at[col], wt.at[col], wc_send.at[0], wc_recv.at[0], mate))
 
     for j in range(1, ycount):
         part = wt.at[yfrom(j)]
@@ -206,7 +206,7 @@
     for t in range(chunks):
         for j in range(1, ycount):
             p2(t, j).wait_recv()
-        for k in range(rows - 1, 0, -1):
+        for k in range(1, rows):
             to = zpeer(k)
             total = f32(obuf[t, core, ypos, to]) + f32(r1[t, ypos, to])
             for j in range(1, ycount):
@@ -218,7 +218,7 @@
         total = f32(obuf[t, core, ypos, row]) + f32(r1[t, ypos, row])
         for j in range(1, ycount):
             total = total + f32(r2[t, j, row])
-        for k in range(rows - 1, 0, -1):
+        for k in range(1, rows):
             p3(t, k).wait_recv()
             total = total + f32(r3[t, k])
         out[:, span] = (f32(tok[col, row, :, span]) + total).astype(jnp.bfloat16)

time: 29.3 us -> 28.8 us (0.983)
  Pallas kernels: 28.5 us -> 28 us
    pallas_call x1, Pallas kernels: 28.5 us -> 28 us  [relay(): pl.pallas_call(functools.partial(relay_kernel, sections, rows, columns, c...]
where the time goes in v4:
time: 28.8 us; the launch traced here: 28.6 us
  Pallas kernels  28 us (97%)
  local copies, waits for them, and re-layouts  0.62 us (2%)
    pallas_call x1, Pallas kernels, relay(): pl.pallas_call(functools.partial(relay_kernel, sections, rows, columns, c...  28 us
    unnamed x1, local copies, waits for them, and re-layouts  0.62 us

profile of v4, /device:TPU:0, one launch (start us, length us, event | category | flops | bytes accessed | tf_op | source)
XLA Modules:
  0.0 28.6 jit_solution(4308708754236401736)
XLA Ops:
  0.0 28.0 %shard_map.73 = bf16[8,2048]{1,0:T(8,128)(2,1)S(1)} custom-call(bf16[8,2048]{1,0:T(8,128)(2,1)} %bitcast.13, s32[8,8]{1,0:T(8,128)} %bitcast.14, f32[8,8]{1,0:T(8,128)} %bitcast.15, bf16[4,4,8,1536]{3,2,1,0:T(8,128)(2,1)} %bitcast.12, bf16[768,2048]{1,0:T(8,128)(2,1)} %bitcast.9, bf16[768,2048]{1,0:T(8,128)(2,1)} %bitcast.10, bf16[768,2048]{1,0:T(8,128)(2,1)} %bitcast.11), custom_call_target="tpu_custom_call" | custom-call | tf_op jit(solution)/shard_map/pallas_call | solution.py:241
  28.0 0.6 %copy.9 = bf16[1,8,2048]{2,1,0:T(8,128)(2,1)} copy(bf16[1,8,2048]{2,1,0:T(8,128)(2,1)S(1)} %bitcast.8) | data formatting | bytes 65536
